TPU v7x, 128 devices: a whole 4x4x4 slice. The times are simulated.
128 devices in a mesh: row: 8 (over z, core), col: 16 (over y, x).
Axes of the slice: x: 4, y: 4, z: 4, core: 2. Of those that a mesh axis runs over, the one named last changes fastest.
Arguments:
- left_amps: bfloat16 [8192, 8192], P('row', 'col'), may hold values from -6 to 6
- right_ints: bfloat16 [8192, 16384], P('row', 'col'), may hold values from -0.0625 to 0.0625
- left_mask: int32 [64, 64], P('row', 'col'), may hold values from 0 to 1, as said below
- right_mask: int32 [64, 128], P('row', 'col'), may hold values from 0 to 1, as said below
- result_mask: int32 [64, 128], P('row', 'col'), may hold values from 0 to 1, as said below
Outputs:
- pair_major: bfloat16 [128, 1048576], P(None, ('row', 'col'))
Inputs may be any that keep to these rules, and one draw needn't show every extreme that they name: `left_mask`: a tile is kept (1) or left out (0). `right_mask`: a tile is kept (1) or left out (0). `result_mask`: a tile is kept (1) or left out (0).
All inputs are finite; a program needn't handle non-finite values.
Results may differ from a plain program's by a relative error of at most 0.001.
Values may be sent and summed in bfloat16 or wider, within the bound.
A program may use at most 128 MiB of HBM per device.

v0:
```python
import jax
import jax.numpy as jnp
from jax import lax
from jax.sharding import PartitionSpec as P

TILE = 128


def expand(values, mask):
    rows, cols = values.shape
    tiled = values.reshape(rows // TILE, TILE, cols // TILE, TILE)
    kept = tiled * mask.astype(values.dtype)[:, None, :, None]
    return kept.reshape(rows, cols)


def local(left_amps, right_ints, left_mask, right_mask, result_mask):
    masked_left = expand(left_amps, left_mask)
    masked_right = expand(right_ints, right_mask)
    rows_here = masked_left.shape[0]
    cols_here = masked_right.shape[1]
    whole_left = lax.all_gather(masked_left, "col", axis=1, tiled=True)
    product = jnp.dot(
        whole_left,
        lax.all_gather(masked_right, "row", axis=0, tiled=True),
        preferred_element_type=jnp.float32,
    )
    kept = expand(product, result_mask).astype(jnp.bfloat16)
    n_row = lax.axis_size("row")
    n_col = lax.axis_size("col")
    owners = n_row * n_col
    share = rows_here * cols_here // owners
    pieces = kept.reshape(owners, share)
    return lax.all_to_all(pieces, ("row", "col"), split_axis=0, concat_axis=0, tiled=True)


def solution(mesh):
    in_specs = (P("row", "col"), P("row", "col"), P("row", "col"), P("row", "col"), P("row", "col"))
    out_specs = P(None, ("row", "col"))
    return jax.shard_map(local, mesh=mesh, in_specs=in_specs, out_specs=out_specs, check_vma=False)
```

profile of v0, /device:TPU:1, one launch (start us, length us, event | category | flops | bytes accessed | tf_op | source)
XLA Modules:
  0.0 325.5 jit_solution(3875941070786762936)
XLA Ops:
  6.5 0.0 all-gather.5.cloned.1.call-start
  6.5 0.7 convert_element_type.13
  7.2 0.3 mul.36
  7.6 0.0 copy-start.2
  7.6 0.0 copy-start
  7.6 3.3 %bitcast_multiply_fusion.1 = bf16[1024,1024]{1,0:T(8,128)(2,1)} fusion(bf16[1024,1024]{1,0:T(8,128)(2,1)} %param.6, bf16[128,8,8,128]{3,2,1,0:T(8,128)(2,1)S(1)} %bitcast.19), kind=kLoop, calls=%fused_computation.2 | loop fusion | flops 1048576 | bytes 6291456 | tf_op jit(solution)/shard_map/mul | solution.py:12
  10.9 0.0 copy-start.1
  10.9 0.0 all-gather.5.cloned.1.call-update
  10.9 0.0 all-gather.3.cloned.1.call-start
  10.9 0.0 copy-done.2
  11.0 0.1 copy.9
  11.1 0.3 mul.33
  11.4 0.0 copy-done
  11.4 1.2 bitcast_multiply_fusion.2
  12.6 0.0 all-gather.3.cloned.1.call-update
  12.6 0.0 copy-done.1
  12.6 87.2 %all-gather.5.cloned.1.call-done = bf16[8192,1024]{1,0:T(8,128)(2,1)} async-done(((bf16[1024,1024]{1,0:T(8,128)(2,1)}), bf16[8192,1024]{1,0:T(8,128)(2,1)}) %all-gather.5.cloned.1.call-update) | async-done | bytes 16777232 | tf_op jit(solution)/shard_map/all_gather | solution.py:24
  99.9 122.2 %all-gather.3.cloned.1.call-done = bf16[1024,8192]{1,0:T(8,128)(2,1)} async-done(((bf16[1024,512]{1,0:T(8,128)(2,1)}), bf16[1024,8192]{1,0:T(8,128)(2,1)}) %all-gather.3.cloned.1.call-update) | async-done | bytes 16777232 | tf_op jit(solution)/shard_map/all_gather | solution.py:21
  222.1 0.3 mul.39
  222.4 22.4 %fusion = bf16[1024,1024]{1,0:T(8,128)(2,1)S(1)} fusion(f32[128,8,8,128]{3,2,1,0:T(8,128)S(1)} %bitcast.21, bf16[1024,8192]{1,0:T(8,128)(2,1)} %all-gather.3.cloned.1.call-done, bf16[8192,1024]{1,0:T(8,128)(2,1)} %all-gather.5.cloned.1.call-done), kind=kOutput, calls=%fused_computation.1 | convolution fusion | flops 17181966336 | bytes 39845888 | tf_op jit(solution)/shard_map/dot_general | solution.py:22
  244.8 6.5 %all_to_all.11 = bf16[128,1,8192]{2,1,0:T(2,128)(2,1)} reshape(bf16[1024,1024]{1,0:T(8,128)(2,1)S(1)} %fusion) | data formatting | bytes 4194304 | tf_op jit(solution)/shard_map/all_to_all | solution.py:33
  251.3 0.5 broadcast.6
  251.8 13.2 %reduce = bf16[128,8192]{1,0:T(8,128)(2,1)S(1)} reduce(bf16[128,1,8192]{2,1,0:T(2,128)(2,1)} %all_to_all.11, bf16[]{:T(256)} %broadcast.6), dimensions={1}, to_apply=%all_to_all.11.reduce_sub_computation | reduce | bytes 4194306 | tf_op jit(solution)/shard_map/all_to_all | solution.py:33
  265.1 2.8 reshape.16
  267.8 38.3 %all_to_all.13 = bf16[128,2,4096]{2,1,0:T(2,128)(2,1)S(1)} all-to-all(bf16[128,2,4096]{2,1,0:T(2,128)(2,1)} %reshape.16), channel_id=1, replica_groups=mesh['row'=8,'col'=16] {'row','col'}, dimensions={0} | all-to-all | bytes 4194304 | tf_op jit(solution)/shard_map/all_to_all | solution.py:33
  306.1 6.7 %reshape.17 = bf16[128,1,8192]{2,1,0:T(2,128)(2,1)} reshape(bf16[128,2,4096]{2,1,0:T(2,128)(2,1)S(1)} %all_to_all.13) | data formatting | bytes 4194304
  312.8 5.8 %copy.19 = bf16[128,1,8192]{2,0,1:T(8,128)(2,1)} copy(bf16[128,1,8192]{2,1,0:T(2,128)(2,1)} %reshape.17) | data formatting | bytes 4194304
  (2 shorter events, 0.0 us)
Async XLA Ops:
  6.5 93.3 %all-gather.5.cloned.1.call-start = ((), (), s32[]{:S(2)}) async-start(), calls=%async_computation.2 | async-start | bytes 18874368 | tf_op jit(solution)/shard_map/all_gather | solution.py:24
  7.6 3.4 %copy-start.2 = (s32[8,4]{0,1:T(4,128)S(1)}, s32[8,4]{0,1:T(4,128)}, u32[]{:S(2)}) copy-start(s32[8,4]{0,1:T(4,128)} %param.7) | copy-start | bytes 388
  7.6 3.8 %copy-start = (bf16[1024,512]{1,0:T(8,128)(2,1)S(1)}, bf16[1024,512]{1,0:T(8,128)(2,1)}, u32[]{:S(2)}) copy-start(bf16[1024,512]{1,0:T(8,128)(2,1)} %param.5) | copy-start | bytes 3145732
  10.9 1.7 copy-start.1
  10.9 211.2 %all-gather.3.cloned.1.call-start = ((), (), s32[]{:S(2)}) async-start(), calls=%async_computation.1 | async-start | bytes 17825792 | tf_op jit(solution)/shard_map/all_gather | solution.py:21
Sparse Core Ops, SparseCore 0:
  11.0 88.8 all-gather.4
  102.0 120.0 all-gather.2
where the time goes:
time: 326 us; the launch traced here: 325 us
  waiting for transfers between devices  209 us (64%)
  blocking collectives  38.3 us (12%)
  local copies, waits for them, and re-layouts  23.4 us (7%)
  matrix products  22.4 us (7%)
  other arithmetic  18.4 us (6%)
  between operations  13.5 us (4%)
    all_gather x1, waiting for transfers between devices, local(): whole_left = lax.all_gather(masked_left, 'col', axis=1, tiled=True)  122 us
    all_gather x1, waiting for transfers between devices, local(): lax.all_gather(masked_right, 'row', axis=0, tiled=True)  87.2 us
    all_to_all x1, blocking collectives, local(): lax.all_to_all(pieces, ('row', 'col'), split_axis=0, concat_axis=0, tiled...  38.3 us
    dot_general x1, matrix products, local(): jnp.dot(whole_left, lax.all_gather(masked_right, 'row', axis=0, tiled=Tru...  22.4 us
    unnamed x9, local copies, waits for them, and re-layouts  15.3 us
    all_to_all x1, other arithmetic, local(): lax.all_to_all(pieces, ('row', 'col'), split_axis=0, concat_axis=0, tiled...  13.2 us
    all_to_all x2, local copies, waits for them, and re-layouts, local(): lax.all_to_all(pieces, ('row', 'col'), split_axis=0, concat_axis=0, tiled...  7.03 us
  transfers between devices with their start and end apart: 2, of which 2 were waited for; matrix products, arithmetic and copies ran while one was open for 0% of the time, Pallas kernels for 0%

commit v1 on v0

--- a/solution.py
+++ b/solution.py
@@ -4,6 +4,28 @@
 from jax.sharding import PartitionSpec as P
 
 TILE = 128
+
+
+def joined_along(tiles, dim):
+    lengths = list(tiles.shape[1:])
+    lengths[dim] *= tiles.shape[0]
+    return jnp.moveaxis(tiles, 0, dim).reshape(lengths)
+
+
+def collect(value, axis, dim):
+    size = lax.axis_size(axis)
+    pairs = [(i, (i + 1) % size) for i in range(size)]
+    back = [(b, a) for a, b in pairs]
+    lower, upper = ([], [])
+    for lap in range(size - 1):
+        if lap % 2 == 0:
+            lower.append(lax.ppermute(lower[-1] if lower else value, axis, pairs))
+        else:
+            upper.append(lax.ppermute(upper[-1] if upper else value, axis, back))
+    blocks = jnp.stack([*lower[::-1], value, *upper])
+    shift = lax.axis_index(axis) - len(lower)
+    blocks = blocks[(jnp.arange(size) - shift) % size]
+    return joined_along(blocks, dim)
 
 
 def expand(values, mask):
@@ -20,9 +42,7 @@
     cols_here = masked_right.shape[1]
     whole_left = lax.all_gather(masked_left, "col", axis=1, tiled=True)
     product = jnp.dot(
-        whole_left,
-        lax.all_gather(masked_right, "row", axis=0, tiled=True),
-        preferred_element_type=jnp.float32,
+        whole_left, collect(masked_right, "row", 0), preferred_element_type=jnp.float32
     )
     kept = expand(product, result_mask).astype(jnp.bfloat16)
     n_row = lax.axis_size("row")

time: 326 us -> 296 us (0.908)
  waiting for transfers between devices: 209 us -> 88.7 us
  local copies, waits for them, and re-layouts: 23.4 us -> 77.4 us
  other arithmetic: 18.4 us -> 32.5 us
  starting transfers between devices: 0.04 us -> 14 us
  blocking collectives: 38.3 us -> 42.3 us
  matrix products: 22.4 us -> 26.3 us
    all_gather x1, waiting for transfers between devices: 122 us -> 0.01 us  [local(): whole_left = lax.all_gather(masked_left, 'col', axis=1, tiled=True)]
    ppermute x0 -> x7, waiting for transfers between devices: none -> 88.7 us  [the longest x4 87.5 us: collect(): lower.append(lax.ppermute(lower[-1] if lower else value, axis, pairs))]
    all_gather x1 -> x0, waiting for transfers between devices: 87.2 us -> none  [local(): lax.all_gather(masked_right, 'row', axis=0, tiled=True)]
    gather x0 -> x3, local copies, waits for them, and re-layouts: none -> 22.5 us  [collect(): blocks = blocks[(jnp.arange(size) - shift) % size]]
    reshape x0 -> x1, local copies, waits for them, and re-layouts: none -> 21.3 us  [joined_along(): return jnp.moveaxis(tiles, 0, dim).reshape(lengths)]
    ppermute x0 -> x7, starting transfers between devices: none -> 14 us  [the longest x4 10.6 us: collect(): lower.append(lax.ppermute(lower[-1] if lower else value, axis, pairs))]
    unnamed x0 -> x1, other arithmetic: none -> 13.7 us
    all_to_all x1 -> x0, other arithmetic: 13.2 us -> none  [local(): lax.all_to_all(pieces, ('row', 'col'), split_axis=0, concat_axis=0, tiled...]
  transfers between devices with their start and end apart: 2 -> 8, of which waited for: 2 -> 6; matrix products, arithmetic and copies ran while one was open for 0% -> 23% of each run, Pallas kernels for 0% -> 0%
where the time goes in v1:
time: 296 us; the launch traced here: 295 us
  waiting for transfers between devices  88.7 us (30%)
  local copies, waits for them, and re-layouts  77.4 us (26%)
  blocking collectives  42.3 us (14%)
  other arithmetic  32.5 us (11%)
  matrix products  26.3 us (9%)
  starting transfers between devices  14 us (5%)
  between operations  13.5 us (5%)
    ppermute x4, waiting for transfers between devices, collect(): lower.append(lax.ppermute(lower[-1] if lower else value, axis, pairs))  87.5 us
    all_to_all x1, blocking collectives, local(): lax.all_to_all(pieces, ('row', 'col'), split_axis=0, concat_axis=0, tiled...  42.3 us
    dot_general x1, matrix products, local(): jnp.dot(whole_left, collect(masked_right, 'row', 0), preferred_element_ty...  26.3 us
    unnamed x20, local copies, waits for them, and re-layouts  23.1 us
    gather x3, local copies, waits for them, and re-layouts, collect(): blocks = blocks[(jnp.arange(size) - shift) % size]  22.5 us
    reshape x1, local copies, waits for them, and re-layouts, joined_along(): return jnp.moveaxis(tiles, 0, dim).reshape(lengths)  21.3 us
    unnamed x1, other arithmetic  13.7 us
    convert_element_type x1, other arithmetic, local(): kept = expand(product, result_mask).astype(jnp.bfloat16)  13.2 us
  transfers between devices with their start and end apart: 8, of which 6 were waited for; matrix products, arithmetic and copies ran while one was open for 23% of the time, Pallas kernels for 0%

profile of v1, /device:TPU:1, one launch (start us, length us, event | category | flops | bytes accessed | tf_op | source)
XLA Modules:
  0.0 294.9 jit_solution(7676039028394510990)
XLA Ops:
  6.5 0.7 convert_element_type.23
  7.7 2.4 bitcast_multiply_fusion.1
  10.1 0.7 convert_element_type.24
  11.1 1.9 bitcast_multiply_fusion
  13.0 3.0 %collective-permute-start = (bf16[1024,1024]{1,0:T(8,128)(2,1)S(1)}, bf16[1024,1024]{1,0:T(8,128)(2,1)S(1)}, u32[]{:S(2)}, u32[]{:S(2)}) collective-permute-start(bf16[1024,1024]{1,0:T(8,128)(2,1)S(1)} %bitcast_multiply_fusion), channel_id=1, source_target_pairs={{0,16},{16,32},{32,48},{48,64},{64,80},{80,96},{96,112},{112,0},{1... | collective-permute-start | bytes 6291464 | tf_op jit(solution)/shard_map/ppermute | solution.py:22
  16.0 23.0 %collective-permute-done = bf16[1024,1024]{1,0:T(8,128)(2,1)S(1)} collective-permute-done((bf16[1024,1024]{1,0:T(8,128)(2,1)S(1)}, bf16[1024,1024]{1,0:T(8,128)(2,1)S(1)}, u32[]{:S(2)}, u32[]{:S(2)}) %collective-permute-start) | collective-permute-done | bytes 2097184 | tf_op jit(solution)/shard_map/ppermute | solution.py:22
  39.0 2.5 collective-permute-start.1
  41.7 22.8 %collective-permute-done.1 = bf16[1024,1024]{1,0:T(8,128)(2,1)S(1)} collective-permute-done((bf16[1024,1024]{1,0:T(8,128)(2,1)S(1)}, bf16[1024,1024]{1,0:T(8,128)(2,1)S(1)}, u32[]{:S(2)}, u32[]{:S(2)}) %collective-permute-start.1) | collective-permute-done | bytes 2097184 | tf_op jit(solution)/shard_map/ppermute | solution.py:22
  64.5 2.5 collective-permute-start.2
  67.3 1.1 collective-permute-start.5
  68.4 21.5 %collective-permute-done.2 = bf16[1024,1024]{1,0:T(8,128)(2,1)} collective-permute-done((bf16[1024,1024]{1,0:T(8,128)(2,1)S(1)}, bf16[1024,1024]{1,0:T(8,128)(2,1)}, u32[]{:S(2)}, u32[]{:S(2)}) %collective-permute-start.2) | collective-permute-done | bytes 2097184 | tf_op jit(solution)/shard_map/ppermute | solution.py:22
  89.9 2.6 collective-permute-start.3
  92.6 0.9 collective-permute-done.5
  93.4 2.2 collective-permute-start.6
  95.6 20.2 %collective-permute-done.3 = bf16[1024,1024]{1,0:T(8,128)(2,1)} collective-permute-done((bf16[1024,1024]{1,0:T(8,128)(2,1)}, bf16[1024,1024]{1,0:T(8,128)(2,1)}, u32[]{:S(2)}, u32[]{:S(2)}) %collective-permute-start.3) | collective-permute-done | bytes 2097184 | tf_op jit(solution)/shard_map/ppermute | solution.py:22
  115.8 1.9 bitcast_dynamic-update-slice_fusion.7
  117.7 1.9 bitcast_dynamic-update-slice_fusion.6
  120.1 1.8 bitcast_dynamic-update-slice_fusion.2
  121.9 1.8 bitcast_dynamic-update-slice_fusion.1
  123.8 6.4 %fusion.2 = (bf16[8,512,1024]{2,1,0:T(8,128)(2,1)}, bf16[8,512,1024]{2,1,0:T(8,128)(2,1)}) fusion(bf16[8,1024,1024]{2,1,0:T(8,128)(2,1)S(1)} %bitcast_dynamic-update-slice_fusion), kind=kLoop, calls=%fused_computation.22 | loop fusion | bytes 33554432 | tf_op jit(solution)/shard_map/gather | solution.py:27
  130.2 8.0 %gather_fusion = bf16[8,512,1024]{2,1,0:T(8,128)(2,1)} fusion(bf16[8,512,1024]{2,1,0:T(8,128)(2,1)} %get-tuple-element.5, s32[1024]{0:T(1024)S(1)} %pad_clamp_fusion), kind=kCustom, calls=%fused_computation | custom fusion | bytes 16777248 | tf_op jit(solution)/shard_map/gather | solution.py:27
  138.3 8.0 %gather_fusion.1 = bf16[8,512,1024]{2,1,0:T(8,128)(2,1)} fusion(bf16[8,512,1024]{2,1,0:T(8,128)(2,1)} %get-tuple-element.6, s32[1024]{0:T(1024)S(1)} %pad_clamp_fusion), kind=kCustom, calls=%fused_computation.1 | custom fusion | bytes 16777248 | tf_op jit(solution)/shard_map/gather | solution.py:27
  146.3 13.7 %pad_maximum_fusion = bf16[8,1024,1024]{2,1,0:T(8,128)(2,1)} fusion(bf16[8,512,1024]{2,1,0:T(8,128)(2,1)} %gather_fusion.1, bf16[8,512,1024]{2,1,0:T(8,128)(2,1)} %gather_fusion), kind=kLoop, calls=%fused_computation.2 | loop fusion | flops 33554432 | bytes 33554432
  160.0 21.3 %copy.16 = bf16[8192,1024]{0,1:T(8,128)(2,1)} copy(bf16[8192,1024]{1,0:T(8,128)(2,1)} %bitcast.44) | data formatting | bytes 33554432 | tf_op jit(solution)/shard_map/reshape | solution.py:12
  181.3 26.3 %multiply_convert_fusion = bf16[8,128,8,128]{3,1,2,0:T(8,128)(2,1)} fusion(bf16[8,128,8192,1]{2,1,3,0:T(8,128)(2,1)} %bitcast.48, bf16[8,128,8192,1]{2,1,0,3:T(8,128)(2,1)} %bitcast.45, f32[8,8]{1,0:T(8,128)S(1)} %convert_element_type.25), kind=kOutput, calls=%fused_computation.3 | convolution fusion | flops 17181966336 | bytes 35651840 | tf_op jit(solution)/shard_map/dot_general | solution.py:44
  207.6 3.0 %copy.17 = bf16[8,128,8,128]{3,2,1,0:T(8,128)(2,1)S(1)} copy(bf16[8,128,8,128]{3,1,2,0:T(8,128)(2,1)} %multiply_convert_fusion) | data formatting | bytes 4194304 | tf_op jit(solution)/shard_map/convert_element_type | solution.py:47
  210.5 6.2 %convert_element_type.28 = bf16[128,1,8192]{2,1,0:T(2,128)(2,1)} reshape(bf16[8,128,8,128]{3,2,1,0:T(8,128)(2,1)S(1)} %copy.17) | data formatting | bytes 4194304 | tf_op jit(solution)/shard_map/convert_element_type | solution.py:47
  217.2 13.2 %reduce = bf16[128,8192]{1,0:T(8,128)(2,1)S(1)} reduce(bf16[128,1,8192]{2,1,0:T(2,128)(2,1)} %convert_element_type.28, bf16[]{:T(256)} %broadcast.78), dimensions={1}, to_apply=%convert_element_type.28.reduce_sub_computation | reduce | bytes 4194306 | tf_op jit(solution)/shard_map/convert_element_type | solution.py:47
  230.5 2.8 reshape.105
  233.2 42.3 %all_to_all.9 = bf16[128,2,4096]{2,1,0:T(2,128)(2,1)S(1)} all-to-all(bf16[128,2,4096]{2,1,0:T(2,128)(2,1)} %reshape.105), channel_id=1, replica_groups=mesh['row'=8,'col'=16] {'row','col'}, dimensions={0} | all-to-all | bytes 4194304 | tf_op jit(solution)/shard_map/all_to_all | solution.py:53
  275.6 6.7 %reshape.106 = bf16[128,1,8192]{2,1,0:T(2,128)(2,1)} reshape(bf16[128,2,4096]{2,1,0:T(2,128)(2,1)S(1)} %all_to_all.9) | data formatting | bytes 4194304
  282.3 5.8 %copy.26 = bf16[128,1,8192]{2,0,1:T(8,128)(2,1)} copy(bf16[128,1,8192]{2,1,0:T(2,128)(2,1)} %reshape.106) | data formatting | bytes 4194304
  (27 shorter events, 2.7 us)
Async XLA Ops:
  6.5 86.0 %copy-start.4 = (s32[8,8]{1,0:T(8,128)S(1)}, s32[8,8]{1,0:T(8,128)}, u32[]{:S(2)}) copy-start(s32[8,8]{1,0:T(8,128)} %param.9) | copy-start | bytes 772
  6.5 174.7 %all-gather.2.cloned.1.call-start = ((), (), s32[]{:S(2)}) async-start(), calls=%async_computation.1 | async-start | bytes 17825792 | tf_op jit(solution)/shard_map/all_gather | solution.py:43
  13.0 26.0 %collective-permute-start = (bf16[1024,1024]{1,0:T(8,128)(2,1)S(1)}, bf16[1024,1024]{1,0:T(8,128)(2,1)S(1)}, u32[]{:S(2)}, u32[]{:S(2)}) collective-permute-start(bf16[1024,1024]{1,0:T(8,128)(2,1)S(1)} %bitcast_multiply_fusion), channel_id=1, source_target_pairs={{0,16},{16,32},{32,48},{48,64},{64,80},{80,96},{96,112},{112,0},{1... | collective-permute-start | bytes 6291464 | tf_op jit(solution)/shard_map/ppermute | solution.py:22
  39.0 28.3 %copy-start = (bf16[1024,1024]{1,0:T(8,128)(2,1)}, bf16[1024,1024]{1,0:T(8,128)(2,1)S(1)}, u32[]{:S(2)}) copy-start(bf16[1024,1024]{1,0:T(8,128)(2,1)S(1)} %collective-permute-done) | copy-start | bytes 6291460
  39.0 25.5 %collective-permute-start.1 = (bf16[1024,1024]{1,0:T(8,128)(2,1)S(1)}, bf16[1024,1024]{1,0:T(8,128)(2,1)S(1)}, u32[]{:S(2)}, u32[]{:S(2)}) collective-permute-start(bf16[1024,1024]{1,0:T(8,128)(2,1)S(1)} %collective-permute-done), channel_id=1, source_target_pairs={{0,16},{16,32},{32,48},{48,64},{64,80},{80,96},{96,112},{112,0},{1... | collective-permute-start | bytes 6291464 | tf_op jit(solution)/shard_map/ppermute | solution.py:22
  41.5 25.9 %collective-permute-start.4 = (bf16[1024,1024]{1,0:T(8,128)(2,1)S(1)}, bf16[1024,1024]{1,0:T(8,128)(2,1)}, u32[]{:S(2)}, u32[]{:S(2)}) collective-permute-start(bf16[1024,1024]{1,0:T(8,128)(2,1)S(1)} %bitcast_multiply_fusion), channel_id=1, source_target_pairs={{16,0},{32,16},{48,32},{64,48},{80,64},{96,80},{112,96},{0,112},{1... | collective-permute-start | bytes 6291464 | tf_op jit(solution)/shard_map/ppermute | solution.py:24
  64.5 3.9 %copy-start.2 = (bf16[1024,1024]{1,0:T(8,128)(2,1)}, bf16[1024,1024]{1,0:T(8,128)(2,1)S(1)}, u32[]{:S(2)}) copy-start(bf16[1024,1024]{1,0:T(8,128)(2,1)S(1)} %collective-permute-done.1) | copy-start | bytes 6291460
  64.5 25.5 %collective-permute-start.2 = (bf16[1024,1024]{1,0:T(8,128)(2,1)S(1)}, bf16[1024,1024]{1,0:T(8,128)(2,1)}, u32[]{:S(2)}, u32[]{:S(2)}) collective-permute-start(bf16[1024,1024]{1,0:T(8,128)(2,1)S(1)} %collective-permute-done.1), channel_id=1, source_target_pairs={{0,16},{16,32},{32,48},{48,64},{64,80},{80,96},{96,112},{112,0},{1... | collective-permute-start | bytes 6291464 | tf_op jit(solution)/shard_map/ppermute | solution.py:22
  67.3 26.1 %collective-permute-start.5 = (bf16[1024,1024]{1,0:T(8,128)(2,1)}, bf16[1024,1024]{1,0:T(8,128)(2,1)}, u32[]{:S(2)}, u32[]{:S(2)}) collective-permute-start(bf16[1024,1024]{1,0:T(8,128)(2,1)} %collective-permute-done.4), channel_id=1, source_target_pairs={{16,0},{32,16},{48,32},{64,48},{80,64},{96,80},{112,96},{0,112},{1... | collective-permute-start | bytes 6291464 | tf_op jit(solution)/shard_map/ppermute | solution.py:24
  89.9 25.9 %collective-permute-start.3 = (bf16[1024,1024]{1,0:T(8,128)(2,1)}, bf16[1024,1024]{1,0:T(8,128)(2,1)}, u32[]{:S(2)}, u32[]{:S(2)}) collective-permute-start(bf16[1024,1024]{1,0:T(8,128)(2,1)} %collective-permute-done.2), channel_id=1, source_target_pairs={{0,16},{16,32},{32,48},{48,64},{64,80},{80,96},{96,112},{112,0},{1... | collective-permute-start | bytes 6291464 | tf_op jit(solution)/shard_map/ppermute | solution.py:22
  92.5 27.0 %copy-start.3 = (bf16[1024,1024]{1,0:T(8,128)(2,1)S(1)}, bf16[1024,1024]{1,0:T(8,128)(2,1)}, u32[]{:S(2)}) copy-start(bf16[1024,1024]{1,0:T(8,128)(2,1)} %copy-done.2) | copy-start | bytes 6291460
  92.5 27.2 %copy-start.1 = (bf16[1024,1024]{1,0:T(8,128)(2,1)S(1)}, bf16[1024,1024]{1,0:T(8,128)(2,1)}, u32[]{:S(2)}) copy-start(bf16[1024,1024]{1,0:T(8,128)(2,1)} %copy-done) | copy-start | bytes 6291460
  93.4 30.2 %collective-permute-start.6 = (bf16[1024,1024]{1,0:T(8,128)(2,1)}, bf16[1024,1024]{1,0:T(8,128)(2,1)S(1)}, u32[]{:S(2)}, u32[]{:S(2)}) collective-permute-start(bf16[1024,1024]{1,0:T(8,128)(2,1)} %collective-permute-done.5), channel_id=1, source_target_pairs={{16,0},{32,16},{48,32},{64,48},{80,64},{96,80},{112,96},{0,112},{1... | collective-permute-start | bytes 6291464 | tf_op jit(solution)/shard_map/ppermute | solution.py:24
Sparse Core Ops, SparseCore 0:
  10.2 123.2 all-gather.1
